TPU v7x, 32 devices: a whole 2x2x4 slice. The times are simulated.
32 devices in a mesh: gx: 4 (over z), gy: 8 (over y, x, core).
Axes of the slice: x: 2, y: 2, z: 4, core: 2. Of those that a mesh axis runs over, the one named last changes fastest.
Arguments:
- operator_blocks: bfloat16 [256, 6, 256, 256], P(('gx', 'gy')), may hold values from -0.15625 to 0.15625
- local_columns: int32 [256, 2], P(('gx', 'gy')), may hold values from 0 to 7
- remote_columns: int32 [256, 4], P(('gx', 'gy')), may hold values from 8 to 17
- match_slots: int32 [256, 6, 2], P(('gx', 'gy')), may hold values from 0 to 2
- tentative: bfloat16 [256, 2, 256, 256], P(('gx', 'gy')), may hold values from -1.5 to 1.5
- inverse_diagonal: bfloat16 [256, 256, 256], P(('gx', 'gy')), may hold values from -0.375 to 0.375
- peer_sends: int32 [32, 8], P(('gx', 'gy')), may hold values from 0 to 7
- slab_sends: int32 [32, 2], P(('gx', 'gy')), may hold values from 0 to 7
- coarse_slots: int32 [256, 2, 2], P(('gx', 'gy')), may hold values from 0 to 47, as said below
Outputs:
- smoothed: bfloat16 [256, 2, 256, 256], P(('gx', 'gy'))
- coarse_operator: bfloat16 [192, 256, 256], P(('gx', 'gy'))
Inputs may be any that keep to these rules, and one draw needn't show every extreme that they name: `match_slots`: the value 2 stands for no matching block. `coarse_slots`: no two partial blocks of one device name the same coarse block; coarse block c of a slab belongs to the device of gy index c // 6.
All inputs are finite; a program needn't handle non-finite values.
Results may differ from a plain program's by a relative error of at most 0.012.
Values may be sent and summed in bfloat16 or wider, within the bound.
A program may use at most 128 MiB of HBM per device.

v0:
```python
import functools

import jax
import jax.numpy as jnp
from jax import lax
from jax.experimental import pallas as pl
from jax.experimental.pallas import tpu as pltpu
from jax.sharding import PartitionSpec as P

MESH = pl.DeviceIdType.MESH


def gather_order(me, group, owned, shape):
    bits = group.bit_length() - 1
    at = lax.broadcasted_iota(jnp.int32, (group * owned, *shape), 0)
    place = at // owned
    high = place // (group // 2)
    odd = (high + me) % 2
    other = high
    for step in range(1, bits):
        bit = (place >> (bits - 1 - step)) & 1
        other = other | jnp.where(odd == 0, bit << step, bit << (bits - step))
    return (me ^ other) * owned + at % owned


def kernel(
    dims,
    local_ref,
    remote_ref,
    match_ref,
    peer_ref,
    slab_ref,
    inverse_ref,
    operator_hbm,
    tentative_hbm,
    diagonal_hbm,
    smooth_hbm,
    coarse_ref,
    operator,
    diagonal,
    own_a,
    own_b,
    rem_a,
    rem_b,
    rem_c,
    send,
    local_sum,
    image,
    *rest,
):
    slabs, group, rows, kl, ko, kp, peers, halo, owned = dims
    bits = group.bit_length() - 1
    landed = rest[:bits]
    load_sem, out_sem, send_sem, recv_sem, slab_send_sem, slab_recv_sem, half_send_sem, half_recv_sem = rest[bits:]
    width = operator.shape[-1]
    gx = lax.axis_index("gx")
    me = lax.axis_index("gy")
    has_below = gx > 0
    has_above = gx < slabs - 1
    own_zero = rows * kp
    rem_zero = (group * peers + 2 * halo) * kp
    span = peers * kp
    slab_span = halo * kp
    slab_at = group * span
    send_slab_at = group * span

    load_rows = pltpu.make_async_copy(tentative_hbm, own_a.at[pl.ds(0, own_zero)], load_sem.at[0])
    load_rows.start()
    load_operator = pltpu.make_async_copy(operator_hbm, operator, load_sem.at[1])
    load_operator.start()
    load_diagonal = pltpu.make_async_copy(diagonal_hbm, diagonal, load_sem.at[2])
    load_diagonal.start()

    barrier = pltpu.get_barrier_semaphore()

    def greet(offset, carry):
        pl.semaphore_signal(
            barrier, inc=1, device_id=(gx, (me + offset) % group), device_id_type=MESH
        )
        return carry

    lax.fori_loop(1, group, greet, 0)

    @pl.when(has_below)
    def _():
        pl.semaphore_signal(barrier, inc=1, device_id=(gx - 1, me), device_id_type=MESH)

    @pl.when(has_above)
    def _():
        pl.semaphore_signal(barrier, inc=1, device_id=(gx + 1, me), device_id_type=MESH)

    zero = jnp.zeros((width, width), jnp.bfloat16)
    own_a[own_zero] = zero
    own_b[own_zero] = zero
    rem_a[rem_zero] = zero
    rem_b[rem_zero] = zero
    rem_c[rem_zero] = zero
    image[own_zero] = zero
    neighbours = jnp.where(has_below, 1, 0) + jnp.where(has_above, 1, 0)
    pl.semaphore_wait(barrier, group - 1 + neighbours)

    load_rows.wait()

    def stage(own, row, buffer, at):
        for n in range(kp):
            buffer[at + n] = own[row * kp + n]

    def peer_copy(step, rem, offset):
        target = (me + offset) % group
        return pltpu.make_async_remote_copy(
            src_ref=send.at[pl.ds(offset * span, span)],
            dst_ref=rem.at[pl.ds(me * span, span)],
            send_sem=send_sem.at[step, offset],
            recv_sem=recv_sem.at[step, offset],
            device_id=(gx, target),
            device_id_type=MESH,
        )

    def slab_copy(step, rem, way):
        return pltpu.make_async_remote_copy(
            src_ref=send.at[pl.ds(send_slab_at + way * slab_span, slab_span)],
            dst_ref=rem.at[pl.ds(slab_at + way * slab_span, slab_span)],
            send_sem=slab_send_sem.at[step, way],
            recv_sem=slab_recv_sem.at[step, way],
            device_id=(gx + 1 - 2 * way, me),
            device_id_type=MESH,
        )

    rems = (rem_a, rem_b, rem_c)

    def post_rows(step, rows_of):
        rem = rems[step]

        def post(turn, carry):
            offset = 1 + (2 * turn + 1) % (group - 1)
            target = (me + offset) % group
            for p in range(peers):
                values = rows_of(peer_ref[0, target * peers + p])
                for n in range(kp):
                    send[offset * span + p * kp + n] = values[n]
            peer_copy(step, rem, offset).start()
            return carry

        lax.fori_loop(0, group - 1, post, 0)
        for way, present in enumerate((has_above, has_below)):

            @pl.when(present)
            def _():
                for h in range(halo):
                    values = rows_of(slab_ref[0, way * halo + h])
                    for n in range(kp):
                        send[send_slab_at + way * slab_span + h * kp + n] = values[n]
                slab_copy(step, rem, way).start()

    post_rows(0, lambda row: [own_a[row * kp + n] for n in range(kp)])

    for step in range(3):
        own, after = (own_a, own_b) if step % 2 == 0 else (own_b, own_a)
        rem = rems[step]
        for p in range(peers):
            stage(own, peer_ref[0, me * peers + p], rem, me * span + p * kp)

        if step == 0:
            load_operator.wait()
        if step == 2:
            store_rows = pltpu.make_async_copy(own.at[pl.ds(0, own_zero)], smooth_hbm, out_sem)
            store_rows.start()

        def local_row(row, carry):
            for n in range(kp):
                value = None
                for k in range(kl):
                    match = match_ref[k, n, row]
                    at = jnp.where(match == kp, own_zero, local_ref[k, row] * kp + match)
                    term = jnp.dot(operator[row, k], own[at], preferred_element_type=jnp.float32)
                    value = term if value is None else value + term
                local_sum[row * kp + n] = value
            return carry

        lax.fori_loop(0, rows, local_row, 0)
        if step == 0:
            load_diagonal.wait()

        def finish(offset, carry):
            peer_copy(step, rem, offset).wait()
            return carry

        lax.fori_loop(1, group, finish, 0)
        for way, (sends, receives) in enumerate(((has_above, has_below), (has_below, has_above))):

            @pl.when(sends)
            def _():
                slab_copy(step, rem, way).wait_send()

            @pl.when(receives)
            def _():
                slab_copy(step, rem, way).wait_recv()

        def images_of(row):
            images = []
            for n in range(kp):
                value = local_sum[row * kp + n]
                for k in range(ko):
                    match = match_ref[kl + k, n, row]
                    source = jnp.maximum(remote_ref[k, row] - rows, 0)
                    from_below = (source >= group * peers) & (source < group * peers + halo)
                    from_above = source >= group * peers + halo
                    absent = (match == kp) | (from_below & (gx == 0)) | (from_above & (gx == slabs - 1))
                    at = jnp.where(absent, rem_zero, source * kp + match)
                    value += jnp.dot(
                        operator[row, kl + k], rem[at], preferred_element_type=jnp.float32
                    )
                images.append(value.astype(jnp.bfloat16))
            return images

        def smoothed_row(row):
            values = []
            for n, image in enumerate(images_of(row)):
                update = jnp.dot(diagonal[row], image, preferred_element_type=jnp.float32)
                before = own[row * kp + n].astype(jnp.float32)
                values.append((before - update).astype(jnp.bfloat16))
            return values

        def own_row(row, carry):
            for n, value in enumerate(smoothed_row(row)):
                after[row * kp + n] = value
            return carry

        def image_row(row, carry):
            for n, value in enumerate(images_of(row)):
                image[row * kp + n] = value
            return carry

        if step < 2:
            post_rows(step + 1, smoothed_row)
            lax.fori_loop(0, rows, own_row, 0)
        else:
            lax.fori_loop(0, rows, image_row, 0)

    core = me % 2
    total_at = group * owned // 2

    def partner(step):
        def flip(bit):
            return me + bit * (1 - 2 * ((me // bit) % 2))

        if step == 0:
            return flip(1)
        return (1 - core) * flip(1 << step) + core * flip(1 << (bits - step))

    grain = owned // 2 if owned % 2 == 0 else owned
    half = group * owned // 2

    def partial_at(place):
        named = inverse_ref[place]
        block = lax.dot_general(
            own_a[named // kp],
            image[named // (kp * kp) * kp + named % kp],
            (((0,), (0,)), ((), ())),
            preferred_element_type=jnp.float32,
        )
        return block.astype(jnp.bfloat16)

    def half_copy(step, chunk):
        at = chunk * grain
        source = at if step == 0 else total_at + (half >> step) + at
        return pltpu.make_async_remote_copy(
            src_ref=rem_a.at[pl.ds(source, grain)],
            dst_ref=landed[step].at[pl.ds(at, grain)],
            send_sem=half_send_sem.at[step, chunk],
            recv_sem=half_recv_sem.at[step, chunk],
            device_id=(gx, partner(step)),
            device_id_type=MESH,
        )

    def send_chunk(chunk):
        def fill(j, carry):
            rem_a[chunk * grain + j] = partial_at(half + chunk * grain + j)
            return carry

        lax.fori_loop(0, grain, fill, 0)
        half_copy(0, chunk).start()

    def add_chunk(step, chunk):
        last = step == bits - 1
        chunks = (half >> step) // grain
        half_copy(step, chunk).wait_recv()

        def add(j, carry):
            at = chunk * grain + j
            mine = partial_at(at) if step == 0 else rem_a[total_at + at]
            value = mine.astype(jnp.float32) + landed[step][at].astype(jnp.float32)
            if last:
                coarse_ref[at] = value.astype(jnp.bfloat16)
            else:
                rem_a[total_at + at] = value.astype(jnp.bfloat16)
            return carry

        lax.fori_loop(0, grain, add, 0)
        if not last and chunk >= chunks // 2:
            half_copy(step + 1, chunk - chunks // 2).start()

    chunks = half // grain
    for chunk in reversed(range(chunks)):
        send_chunk(chunk)
        if chunk + 1 < chunks:
            add_chunk(0, chunk + 1)
    add_chunk(0, 0)
    for step in range(1, bits):
        for chunk in reversed(range((half >> step) // grain)):
            add_chunk(step, chunk)
    for step in range(bits):
        for chunk in range((half >> step) // grain):
            half_copy(step, chunk).wait_send()
    store_rows.wait()


def body(
    operator_blocks,
    local_columns,
    remote_columns,
    match_slots,
    tentative,
    inverse_diagonal,
    peer_sends,
    slab_sends,
    coarse_slots,
):
    slabs = lax.axis_size("gx")
    group = lax.axis_size("gy")
    rows, kp, width = tentative.shape[:3]
    kl, ko = local_columns.shape[1], remote_columns.shape[1]
    peers = peer_sends.shape[1] // group
    halo = slab_sends.shape[1] // 2
    owned = (3 * rows * kp * kp // 2 + group - 1) // group
    bits = group.bit_length() - 1
    count = rows * kp * kp
    dims = (slabs, group, rows, kl, ko, kp, peers, halo, owned)

    named = coarse_slots.transpose(1, 2, 0)
    slots = gather_order(lax.axis_index("gy"), group, owned, named.shape)
    which = [lax.broadcasted_iota(jnp.int32, slots.shape, axis) for axis in (1, 2, 3)]
    which = (which[2] * kp + which[0]) * kp + which[1] - count
    inverse = count + jnp.sum(
        jnp.where(slots == named[None], which, 0), axis=(1, 2, 3), dtype=jnp.int32
    )

    def blocks(n, dtype=jnp.bfloat16):
        return pltpu.VMEM((n, width, width), dtype)

    smem = pl.BlockSpec(memory_space=pltpu.SMEM)
    anywhere = pl.BlockSpec(memory_space=pl.ANY)
    half = group * owned // 2
    remote_count = (group * peers + 2 * halo) * kp
    smoothed, coarse = pl.pallas_call(
        functools.partial(kernel, dims),
        out_shape=(
            jax.ShapeDtypeStruct((rows * kp, width, width), jnp.bfloat16),
            jax.ShapeDtypeStruct((owned, width, width), jnp.bfloat16),
        ),
        in_specs=[smem] * 6 + [anywhere] * 3,
        out_specs=(anywhere, pl.BlockSpec(memory_space=pltpu.VMEM)),
        scratch_shapes=[
            pltpu.VMEM(operator_blocks.shape, jnp.bfloat16),
            blocks(rows),
            blocks(rows * kp + 1),
            blocks(rows * kp + 1),
            blocks(max(remote_count + 1, 2 * half)),
            blocks(remote_count + 1),
            blocks(remote_count + 1),
            blocks(remote_count),
            blocks(rows * kp, jnp.float32),
            blocks(rows * kp + 1),
            *[blocks(half >> step) for step in range(bits)],
            pltpu.SemaphoreType.DMA((3,)),
            pltpu.SemaphoreType.DMA,
            pltpu.SemaphoreType.DMA((3, group)),
            pltpu.SemaphoreType.DMA((3, group)),
            pltpu.SemaphoreType.DMA((3, 2)),
            pltpu.SemaphoreType.DMA((3, 2)),
            pltpu.SemaphoreType.DMA((bits, group)),
            pltpu.SemaphoreType.DMA((bits, group)),
        ],
        compiler_params=pltpu.CompilerParams(
            collective_id=0, has_side_effects=True, vmem_limit_bytes=67_000_000
        ),
    )(
        local_columns.T,
        remote_columns.T,
        match_slots.transpose(1, 2, 0),
        peer_sends,
        slab_sends,
        inverse,
        operator_blocks,
        tentative.reshape(rows * kp, width, width),
        inverse_diagonal,
    )
    return smoothed.reshape(tentative.shape), coarse


def solution(mesh):
    placed = (
        P(("gx", "gy"), None, None, None),
        P(("gx", "gy"), None),
        P(("gx", "gy"), None),
        P(("gx", "gy"), None, None),
        P(("gx", "gy"), None, None, None),
        P(("gx", "gy"), None, None),
        P(("gx", "gy"), None),
        P(("gx", "gy"), None),
        P(("gx", "gy"), None, None),
    )
    return jax.shard_map(
        body,
        mesh=mesh,
        in_specs=placed,
        out_specs=(P(("gx", "gy"), None, None, None), P(("gx", "gy"), None, None)),
        check_vma=False,
    )
```

profile of v0, /device:TPU:0, one launch (start us, length us, event | category | flops | bytes accessed | tf_op | source)
XLA Modules:
  0.0 122.4 jit_solution(15229581540633517843)
XLA Ops:
  0.7 0.8 select_reduce_fusion
  1.5 0.5 broadcast_add_fusion.inverse_ref
  2.0 116.3 %shard_map.104 = (bf16[16,256,256]{2,1,0:T(8,128)(2,1)}, bf16[6,256,256]{2,1,0:T(8,128)(2,1)}) custom-call(s32[2,8]{1,0:T(2,128)} %bitcast.11, s32[4,8]{1,0:T(4,128)} %bitcast.9, s32[6,2,8]{2,1,0:T(2,128)} %bitcast.8, s32[1,8]{1,0:T(1,128)} %peer_ref.1, s32[1,2]{1,0:T(1,128)} %slab_ref.1, s32[48]{0:T(128)} %broadcast_add_fusion.inverse_ref, ...), custom_call_target="tpu_custom_call" | custom-call | tf_op jit(solution)/shard_map/pallas_call | solution.py:355
  118.3 0.0 copy-start
  118.3 3.2 %copy.13 = bf16[8,2,256,256]{3,2,1,0:T(8,128)(2,1)} copy(bf16[8,2,256,256]{3,2,1,0:T(8,128)(2,1)} %bitcast.6) | data formatting | bytes 4194304
  121.5 0.0 copy-done
  121.5 0.9 copy.14
  (4 shorter events, 0.0 us)
Async XLA Ops:
  118.3 3.2 %copy-start = (bf16[6,256,256]{2,1,0:T(8,128)(2,1)S(1)}, bf16[6,256,256]{2,1,0:T(8,128)(2,1)}, u32[]{:S(2)}) copy-start(bf16[6,256,256]{2,1,0:T(8,128)(2,1)} %get-tuple-element.15) | copy-start | bytes 2359300
where the time goes:
time: 123 us; the launch traced here: 122 us
  Pallas kernels  116 us (94%)
  local copies, waits for them, and re-layouts  4.05 us (3%)
  other arithmetic  1.32 us (1%)
    pallas_call x1, Pallas kernels, body(): pl.pallas_call(functools.partial(kernel, dims), out_shape=(jax.ShapeDtype...  116 us
    unnamed x4, local copies, waits for them, and re-layouts  4.05 us

commit v1 on v0

v1 whole, which is shorter than its diff:
```python
import functools

import jax
import jax.numpy as jnp
from jax import lax
from jax.experimental import pallas as pl
from jax.experimental.pallas import tpu as pltpu
from jax.sharding import PartitionSpec as P

MESH = pl.DeviceIdType.MESH
STRIPES = 2


def side_by_side(parts):
    return parts[0] if len(parts) == 1 else jnp.concatenate(parts, axis=1)


def kernel(
    dims,
    local_ref,
    remote_ref,
    match_ref,
    peer_ref,
    slab_ref,
    slots_ref,
    operator_hbm,
    tentative_hbm,
    diagonal_hbm,
    smooth_hbm,
    coarse_ref,
    operator,
    diagonal,
    send,
    local_sum,
    turned,
    partial,
    outgoing,
    total,
    table,
    inverse,
    *rest,
):
    slabs, group, rows, kl, ko, kp, peers, halo, owned = dims
    bits = group.bit_length() - 1
    owns, rest = rest[:STRIPES], rest[STRIPES:]
    rems, rest = (rest[:STRIPES], rest[STRIPES : 2 * STRIPES]), rest[2 * STRIPES :]
    landed = rest[:bits]
    (
        load_sem,
        rows_sem,
        out_sem,
        send_sem,
        recv_sem,
        slab_send_sem,
        slab_recv_sem,
        half_send_sem,
        half_recv_sem,
    ) = rest[bits:]
    width = operator.shape[-1]
    columns = width // STRIPES
    gx = lax.axis_index("gx")
    me = lax.axis_index("gy")
    has_below = gx > 0
    has_above = gx < slabs - 1
    own_zero = rows * kp
    rem_zero = (group * peers + 2 * halo) * kp
    count = rows * kp * kp
    span = peers * kp
    slab_span = halo * kp
    slab_at = group * span

    def load_rows(s):
        return pltpu.make_async_copy(
            tentative_hbm.at[:, :, pl.ds(s * columns, columns)],
            owns[s].at[pl.ds(0, own_zero)],
            rows_sem.at[s],
        )

    for s in range(STRIPES):
        load_rows(s).start()
    load_operator = pltpu.make_async_copy(operator_hbm, operator, load_sem.at[0])
    load_operator.start()
    load_diagonal = pltpu.make_async_copy(diagonal_hbm, diagonal, load_sem.at[1])
    load_diagonal.start()

    barrier = pltpu.get_barrier_semaphore()

    def greet(offset, carry):
        pl.semaphore_signal(
            barrier, inc=1, device_id=(gx, (me + offset) % group), device_id_type=MESH
        )
        return carry

    lax.fori_loop(1, group, greet, 0)

    @pl.when(has_below)
    def _():
        pl.semaphore_signal(barrier, inc=1, device_id=(gx - 1, me), device_id_type=MESH)

    @pl.when(has_above)
    def _():
        pl.semaphore_signal(barrier, inc=1, device_id=(gx + 1, me), device_id_type=MESH)

    zero = jnp.zeros((width, columns), jnp.bfloat16)
    for s in range(STRIPES):
        owns[s][own_zero] = zero
        for rem in rems:
            rem[s][rem_zero] = zero
        partial[s, count] = zero
    neighbours = jnp.where(has_below, 1, 0) + jnp.where(has_above, 1, 0)
    pl.semaphore_wait(barrier, group - 1 + neighbours)

    def peer_copy(step, s, offset):
        return pltpu.make_async_remote_copy(
            src_ref=send.at[s, pl.ds(offset * span, span)],
            dst_ref=rems[step % 2][s].at[pl.ds(me * span, span)],
            send_sem=send_sem.at[step, s, offset],
            recv_sem=recv_sem.at[step, s, offset],
            device_id=(gx, (me + offset) % group),
            device_id_type=MESH,
        )

    def slab_copy(step, s, way):
        at = slab_at + way * slab_span
        return pltpu.make_async_remote_copy(
            src_ref=send.at[s, pl.ds(at, slab_span)],
            dst_ref=rems[step % 2][s].at[pl.ds(at, slab_span)],
            send_sem=slab_send_sem.at[step, s, way],
            recv_sem=slab_recv_sem.at[step, s, way],
            device_id=(gx + 1 - 2 * way, me),
            device_id_type=MESH,
        )

    def post_rows(step, s):
        def post(turn, carry):
            offset = 1 + (2 * turn + 1) % (group - 1)
            target = (me + offset) % group
            for p in range(peers):
                row = peer_ref[0, target * peers + p]
                for n in range(kp):
                    send[s, offset * span + p * kp + n] = owns[s][row * kp + n]
            peer_copy(step, s, offset).start()
            return carry

        lax.fori_loop(0, group - 1, post, 0)
        for way, present in enumerate((has_above, has_below)):

            @pl.when(present)
            def _():
                for h in range(halo):
                    row = slab_ref[0, way * halo + h]
                    for n in range(kp):
                        send[s, slab_at + way * slab_span + h * kp + n] = owns[s][row * kp + n]
                slab_copy(step, s, way).start()

        for p in range(peers):
            row = peer_ref[0, me * peers + p]
            for n in range(kp):
                rems[step % 2][s][me * span + p * kp + n] = owns[s][row * kp + n]

    def arrive(step, s):
        def finish(turn, carry):
            peer_copy(step, s, 1 + (2 * turn + 1) % (group - 1)).wait()
            return carry

        lax.fori_loop(0, group - 1, finish, 0)
        for way, (sends, receives) in enumerate(((has_above, has_below), (has_below, has_above))):

            @pl.when(sends)
            def _():
                slab_copy(step, s, way).wait_send()

            @pl.when(receives)
            def _():
                slab_copy(step, s, way).wait_recv()

    def tabulate(row, carry):
        for k in range(kl):
            for n in range(kp):
                match = match_ref[k, n, row]
                table[k, n, row] = jnp.where(
                    match == kp, own_zero, local_ref[k, row] * kp + match
                )
        for k in range(ko):
            source = jnp.maximum(remote_ref[k, row] - rows, 0)
            from_below = (source >= group * peers) & (source < group * peers + halo)
            from_above = source >= group * peers + halo
            missing = (from_below & (gx == 0)) | (from_above & (gx == slabs - 1))
            for n in range(kp):
                match = match_ref[kl + k, n, row]
                table[kl + k, n, row] = jnp.where(
                    (match == kp) | missing, rem_zero, source * kp + match
                )
        return carry

    def product(row, first, last, rows_of):
        blocks = [operator[row, k] for k in range(first, last)]
        picked = [
            side_by_side([rows_of[table[k, n, row]] for n in range(kp)])
            for k in range(first, last)
        ]
        return jnp.dot(
            jnp.concatenate(blocks, axis=1),
            jnp.concatenate(picked, axis=0),
            preferred_element_type=jnp.float32,
        )

    def local_rows(s):
        def local_row(row, carry):
            local_sum[s, row] = product(row, 0, kl, owns[s])
            return carry

        lax.fori_loop(0, rows, local_row, 0)

    def image_of(row, step, s):
        value = local_sum[s, row] + product(row, kl, kl + ko, rems[step % 2][s])
        return value.astype(jnp.bfloat16)

    def smooth_rows(step, s):
        def smooth_row(row, carry):
            update = jnp.dot(
                diagonal[row], image_of(row, step, s), preferred_element_type=jnp.float32
            )
            for n in range(kp):
                before = owns[s][row * kp + n].astype(jnp.float32)
                after = before - update[:, n * columns : (n + 1) * columns]
                owns[s][row * kp + n] = after.astype(jnp.bfloat16)
            return carry

        lax.fori_loop(0, rows, smooth_row, 0)

    def turn_row(row, carry):
        for n in range(kp):
            for s in range(STRIPES):
                turned[row * kp + n, pl.ds(s * columns, columns)] = owns[s][row * kp + n].T
        return carry

    def partial_rows(step, s):
        def partial_row(row, carry):
            image = image_of(row, step, s)
            for n in range(kp):
                blocks = jnp.dot(
                    turned[row * kp + n], image, preferred_element_type=jnp.float32
                ).astype(jnp.bfloat16)
                for m in range(kp):
                    at = (row * kp + n) * kp + m
                    partial[s, at] = blocks[:, m * columns : (m + 1) * columns]
            return carry

        lax.fori_loop(0, rows, partial_row, 0)

    core = me % 2
    half = group * owned // 2
    grain = owned // 2 if owned % 2 == 0 else owned

    def invert(at, carry):
        place = at // owned
        high = place // (group // 2)
        odd = (high + me) % 2
        other = high
        for step in range(1, bits):
            bit = (place >> (bits - 1 - step)) & 1
            other = other | jnp.where(odd == 0, bit << step, bit << (bits - step))
        slot = (me ^ other) * owned + at % owned
        found = count
        for row in range(rows):
            for n in range(kp):
                for m in range(kp):
                    named = (row * kp + n) * kp + m
                    found = jnp.where(slots_ref[n, m, row] == slot, named, found)
        inverse[at] = found
        return carry

    def partner(step):
        def flip(bit):
            return me + bit * (1 - 2 * ((me // bit) % 2))

        if step == 0:
            return flip(1)
        return (1 - core) * flip(1 << step) + core * flip(1 << (bits - step))

    def half_copy(step, s, chunk):
        at = chunk * grain
        if step == 0:
            source = outgoing.at[s, pl.ds(at, grain)]
        else:
            source = total.at[s, pl.ds((half >> step) + at, grain)]
        return pltpu.make_async_remote_copy(
            src_ref=source,
            dst_ref=landed[step].at[s, pl.ds(at, grain)],
            send_sem=half_send_sem.at[step, s, chunk],
            recv_sem=half_recv_sem.at[step, s, chunk],
            device_id=(gx, partner(step)),
            device_id_type=MESH,
        )

    def send_partials(s):
        def send_chunk(turn, carry):
            chunk = half // grain - 1 - turn
            for j in range(grain):
                at = chunk * grain + j
                outgoing[s, at] = partial[s, inverse[half + at]]
            half_copy(0, s, chunk).start()
            return carry

        lax.fori_loop(0, half // grain, send_chunk, 0)

    def add_partials(step, s):
        last = step == bits - 1
        chunks = (half >> step) // grain

        def add(chunk):
            half_copy(step, s, chunk).wait_recv()
            for j in range(grain):
                at = chunk * grain + j
                mine = partial[s, inverse[at]] if step == 0 else total[s, at]
                value = mine.astype(jnp.float32) + landed[step][s, at].astype(jnp.float32)
                if last:
                    coarse_ref[at, :, s * columns : (s + 1) * columns] = value.astype(jnp.bfloat16)
                else:
                    total[s, at] = value.astype(jnp.bfloat16)

        if last:
            for chunk in reversed(range(chunks)):
                add(chunk)
            return

        def upper(turn, carry):
            chunk = chunks - 1 - turn
            add(chunk)
            half_copy(step + 1, s, chunk - chunks // 2).start()
            return carry

        def lower(turn, carry):
            add(chunks // 2 - 1 - turn)
            return carry

        lax.fori_loop(0, chunks // 2, upper, 0)
        lax.fori_loop(0, chunks // 2, lower, 0)

    stripes = range(STRIPES)
    load_rows(0).wait()
    post_rows(0, 0)
    lax.fori_loop(0, rows, tabulate, 0)
    for s in stripes[1:]:
        load_rows(s).wait()
    load_operator.wait()
    for s in stripes:
        local_rows(s)
    for s in stripes[1:]:
        post_rows(0, s)
    lax.fori_loop(0, group * owned, invert, 0)
    load_diagonal.wait()

    stores = []
    for step in range(2):
        for s in stripes:
            arrive(step, s)
            smooth_rows(step, s)
            post_rows(step + 1, s)
            if step == 1:
                store = pltpu.make_async_copy(
                    owns[s].at[pl.ds(0, own_zero)],
                    smooth_hbm.at[:, :, pl.ds(s * columns, columns)],
                    out_sem.at[s],
                )
                store.start()
                stores.append(store)
            local_rows(s)
    lax.fori_loop(0, rows, turn_row, 0)

    for s in stripes:
        if s > 0:
            add_partials(0, s - 1)
        arrive(2, s)
        partial_rows(2, s)
        send_partials(s)
    for step in range(1, bits):
        add_partials(step, 0)
        add_partials(step - 1, 1)
    add_partials(bits - 1, 1)
    for s in stripes:
        for step in range(bits):
            for chunk in range((half >> step) // grain):
                half_copy(step, s, chunk).wait_send()
    for store in stores:
        store.wait()


def body(
    operator_blocks,
    local_columns,
    remote_columns,
    match_slots,
    tentative,
    inverse_diagonal,
    peer_sends,
    slab_sends,
    coarse_slots,
):
    slabs = lax.axis_size("gx")
    group = lax.axis_size("gy")
    rows, kp, width = tentative.shape[:3]
    kl, ko = local_columns.shape[1], remote_columns.shape[1]
    peers = peer_sends.shape[1] // group
    halo = slab_sends.shape[1] // 2
    owned = (3 * rows * kp * kp // 2 + group - 1) // group
    bits = group.bit_length() - 1
    count = rows * kp * kp
    columns = width // STRIPES
    dims = (slabs, group, rows, kl, ko, kp, peers, halo, owned)

    def blocks(n):
        return pltpu.VMEM((STRIPES, n, width, columns), jnp.bfloat16)

    smem = pl.BlockSpec(memory_space=pltpu.SMEM)
    anywhere = pl.BlockSpec(memory_space=pl.ANY)
    half = group * owned // 2
    remote_count = (group * peers + 2 * halo) * kp
    smoothed, coarse = pl.pallas_call(
        functools.partial(kernel, dims),
        out_shape=(
            jax.ShapeDtypeStruct((rows * kp, width, width), jnp.bfloat16),
            jax.ShapeDtypeStruct((owned, width, width), jnp.bfloat16),
        ),
        in_specs=[smem] * 6 + [anywhere] * 3,
        out_specs=(anywhere, pl.BlockSpec(memory_space=pltpu.VMEM)),
        scratch_shapes=[
            pltpu.VMEM(operator_blocks.shape, jnp.bfloat16),
            pltpu.VMEM((rows, width, width), jnp.bfloat16),
            blocks(remote_count),
            pltpu.VMEM((STRIPES, rows, width, kp * columns), jnp.float32),
            pltpu.VMEM((rows * kp, width, width), jnp.bfloat16),
            blocks(count + 1),
            blocks(half),
            blocks(half),
            pltpu.SMEM((kl + ko, kp, rows), jnp.int32),
            pltpu.SMEM((2 * half,), jnp.int32),
            *[pltpu.VMEM((rows * kp + 1, width, columns), jnp.bfloat16)] * STRIPES,
            *[pltpu.VMEM((remote_count + 1, width, columns), jnp.bfloat16)] * (2 * STRIPES),
            *[blocks(half >> step) for step in range(bits)],
            pltpu.SemaphoreType.DMA((2,)),
            pltpu.SemaphoreType.DMA((STRIPES,)),
            pltpu.SemaphoreType.DMA((STRIPES,)),
            pltpu.SemaphoreType.DMA((3, STRIPES, group)),
            pltpu.SemaphoreType.DMA((3, STRIPES, group)),
            pltpu.SemaphoreType.DMA((3, STRIPES, 2)),
            pltpu.SemaphoreType.DMA((3, STRIPES, 2)),
            pltpu.SemaphoreType.DMA((bits, STRIPES, group)),
            pltpu.SemaphoreType.DMA((bits, STRIPES, group)),
        ],
        compiler_params=pltpu.CompilerParams(
            collective_id=0, has_side_effects=True, vmem_limit_bytes=67_000_000
        ),
    )(
        local_columns.T,
        remote_columns.T,
        match_slots.transpose(1, 2, 0),
        peer_sends,
        slab_sends,
        coarse_slots.transpose(1, 2, 0),
        operator_blocks,
        tentative.reshape(rows * kp, width, width),
        inverse_diagonal,
    )
    return smoothed.reshape(tentative.shape), coarse


def solution(mesh):
    placed = (
        P(("gx", "gy"), None, None, None),
        P(("gx", "gy"), None),
        P(("gx", "gy"), None),
        P(("gx", "gy"), None, None),
        P(("gx", "gy"), None, None, None),
        P(("gx", "gy"), None, None),
        P(("gx", "gy"), None),
        P(("gx", "gy"), None),
        P(("gx", "gy"), None, None),
    )
    return jax.shard_map(
        body,
        mesh=mesh,
        in_specs=placed,
        out_specs=(P(("gx", "gy"), None, None, None), P(("gx", "gy"), None, None)),
        check_vma=False,
    )
```

time: 123 us -> 108 us (0.88)
  Pallas kernels: 116 us -> 103 us
  other arithmetic: 1.32 us -> 0 us
    pallas_call x1, Pallas kernels: 116 us -> 103 us  [body(): pl.pallas_call(functools.partial(kernel, dims), out_shape=(jax.ShapeDtype...]
where the time goes in v1:
time: 108 us
  Pallas kernels  103 us (95%)
  local copies, waits for them, and re-layouts  4.05 us (4%)
    pallas_call x1, Pallas kernels, body(): pl.pallas_call(functools.partial(kernel, dims), out_shape=(jax.ShapeDtype...  103 us
    unnamed x4, local copies, waits for them, and re-layouts  4.05 us

profile of v1, /device:TPU:0, one launch (start us, length us, event | category | flops | bytes accessed | tf_op | source)
XLA Modules:
  0.0 108.1 jit_solution(7777540498413505320)
XLA Ops:
  0.6 103.4 %shard_map.104 = (bf16[16,256,256]{2,1,0:T(8,128)(2,1)}, bf16[6,256,256]{2,1,0:T(8,128)(2,1)}) custom-call(s32[2,8]{1,0:T(2,128)} %bitcast.11, s32[4,8]{1,0:T(4,128)} %bitcast.9, s32[6,2,8]{2,1,0:T(2,128)} %bitcast.8, s32[1,8]{1,0:T(1,128)} %peer_ref.1, s32[1,2]{1,0:T(1,128)} %slab_ref.1, s32[2,2,8]{2,1,0:T(2,128)} %bitcast.10, ...), custom_call_target="tpu_custom_call" | custom-call | tf_op jit(solution)/shard_map/pallas_call | solution.py:420
  104.0 0.0 copy-start
  104.0 3.2 %copy.13 = bf16[8,2,256,256]{3,2,1,0:T(8,128)(2,1)} copy(bf16[8,2,256,256]{3,2,1,0:T(8,128)(2,1)} %bitcast.7) | data formatting | bytes 4194304
  107.2 0.0 copy-done
  107.2 0.9 copy.14
Async XLA Ops:
  104.0 3.2 %copy-start = (bf16[6,256,256]{2,1,0:T(8,128)(2,1)S(1)}, bf16[6,256,256]{2,1,0:T(8,128)(2,1)}, u32[]{:S(2)}) copy-start(bf16[6,256,256]{2,1,0:T(8,128)(2,1)} %get-tuple-element.9) | copy-start | bytes 2359300

commit v2 on v1

--- a/solution.py
+++ b/solution.py
@@ -17,12 +17,12 @@
 
 def kernel(
     dims,
-    local_ref,
-    remote_ref,
-    match_ref,
-    peer_ref,
-    slab_ref,
-    slots_ref,
+    local_hbm,
+    remote_hbm,
+    match_hbm,
+    peer_hbm,
+    slab_hbm,
+    slots_hbm,
     operator_hbm,
     tentative_hbm,
     diagonal_hbm,
@@ -36,6 +36,12 @@
     partial,
     outgoing,
     total,
+    local_ref,
+    remote_ref,
+    match_ref,
+    peer_ref,
+    slab_ref,
+    slots_ref,
     table,
     inverse,
     *rest,
@@ -46,6 +52,7 @@
     rems, rest = (rest[:STRIPES], rest[STRIPES : 2 * STRIPES]), rest[2 * STRIPES :]
     landed = rest[:bits]
     (
+        index_sem,
         load_sem,
         rows_sem,
         out_sem,
@@ -76,7 +83,16 @@
             rows_sem.at[s],
         )
 
-    for s in range(STRIPES):
+    load_peers = pltpu.make_async_copy(peer_hbm, peer_ref, index_sem.at[0])
+    load_slabs = pltpu.make_async_copy(slab_hbm, slab_ref, index_sem.at[1])
+    load_matches = pltpu.make_async_copy(match_hbm, match_ref, index_sem.at[2])
+    load_locals = pltpu.make_async_copy(local_hbm, local_ref, index_sem.at[3])
+    load_remotes = pltpu.make_async_copy(remote_hbm, remote_ref, index_sem.at[4])
+    load_slots = pltpu.make_async_copy(slots_hbm, slots_ref, index_sem.at[5])
+    load_rows(0).start()
+    for load in (load_peers, load_slabs, load_matches, load_locals, load_remotes, load_slots):
+        load.start()
+    for s in range(1, STRIPES):
         load_rows(s).start()
     load_operator = pltpu.make_async_copy(operator_hbm, operator, load_sem.at[0])
     load_operator.start()
@@ -339,8 +355,13 @@
         lax.fori_loop(0, chunks // 2, lower, 0)
 
     stripes = range(STRIPES)
+    load_peers.wait()
+    load_slabs.wait()
     load_rows(0).wait()
     post_rows(0, 0)
+    load_matches.wait()
+    load_locals.wait()
+    load_remotes.wait()
     lax.fori_loop(0, rows, tabulate, 0)
     for s in stripes[1:]:
         load_rows(s).wait()
@@ -349,6 +370,7 @@
         local_rows(s)
     for s in stripes[1:]:
         post_rows(0, s)
+    load_slots.wait()
     lax.fori_loop(0, group * owned, invert, 0)
     load_diagonal.wait()
 
@@ -413,17 +435,36 @@
     def blocks(n):
         return pltpu.VMEM((STRIPES, n, width, columns), jnp.bfloat16)
 
-    smem = pl.BlockSpec(memory_space=pltpu.SMEM)
+    tables = (
+        local_columns.T,
+        remote_columns.T,
+        match_slots.transpose(1, 2, 0),
+        peer_sends,
+        slab_sends,
+        coarse_slots.transpose(1, 2, 0),
+    )
+    arrays = (operator_blocks, tentative.reshape(rows * kp, width, width), inverse_diagonal)
     anywhere = pl.BlockSpec(memory_space=pl.ANY)
     half = group * owned // 2
     remote_count = (group * peers + 2 * halo) * kp
+    scratch_blocks = (
+        (kl + ko + 1) * rows
+        + rows * kp * 2
+        + 3 * remote_count
+        + 2 * rows * kp
+        + count
+        + 4 * half
+        + owned
+        + 4
+    )
+    grant = scratch_blocks * width * width * 2 + 3_000_000
     smoothed, coarse = pl.pallas_call(
         functools.partial(kernel, dims),
         out_shape=(
             jax.ShapeDtypeStruct((rows * kp, width, width), jnp.bfloat16),
             jax.ShapeDtypeStruct((owned, width, width), jnp.bfloat16),
         ),
-        in_specs=[smem] * 6 + [anywhere] * 3,
+        in_specs=[pl.BlockSpec(memory_space=pltpu.HBM)] * 9,
         out_specs=(anywhere, pl.BlockSpec(memory_space=pltpu.VMEM)),
         scratch_shapes=[
             pltpu.VMEM(operator_blocks.shape, jnp.bfloat16),
@@ -434,11 +475,13 @@
             blocks(count + 1),
             blocks(half),
             blocks(half),
+            *[pltpu.SMEM(table.shape, jnp.int32) for table in tables],
             pltpu.SMEM((kl + ko, kp, rows), jnp.int32),
             pltpu.SMEM((2 * half,), jnp.int32),
             *[pltpu.VMEM((rows * kp + 1, width, columns), jnp.bfloat16)] * STRIPES,
             *[pltpu.VMEM((remote_count + 1, width, columns), jnp.bfloat16)] * (2 * STRIPES),
             *[blocks(half >> step) for step in range(bits)],
+            pltpu.SemaphoreType.DMA((len(tables),)),
             pltpu.SemaphoreType.DMA((2,)),
             pltpu.SemaphoreType.DMA((STRIPES,)),
             pltpu.SemaphoreType.DMA((STRIPES,)),
@@ -450,19 +493,9 @@
             pltpu.SemaphoreType.DMA((bits, STRIPES, group)),
         ],
         compiler_params=pltpu.CompilerParams(
-            collective_id=0, has_side_effects=True, vmem_limit_bytes=67_000_000
+            collective_id=0, has_side_effects=True, vmem_limit_bytes=grant
         ),
-    )(
-        local_columns.T,
-        remote_columns.T,
-        match_slots.transpose(1, 2, 0),
-        peer_sends,
-        slab_sends,
-        coarse_slots.transpose(1, 2, 0),
-        operator_blocks,
-        tentative.reshape(rows * kp, width, width),
-        inverse_diagonal,
-    )
+    )(*[pltpu.with_memory_space_constraint(x, pltpu.HBM) for x in tables + arrays])
     return smoothed.reshape(tentative.shape), coarse
 
 

time: 108 us -> 105 us (0.972)
  local copies, waits for them, and re-layouts: 4.05 us -> 2.2 us
    unnamed x4 -> x2, local copies, waits for them, and re-layouts: 4.05 us -> 2.2 us
    pallas_call x1, Pallas kernels: 103 us -> 102 us  [body(): pl.pallas_call(functools.partial(kernel, dims), out_shape=(jax.ShapeDtype...]
where the time goes in v2:
time: 105 us
  Pallas kernels  102 us (97%)
  local copies, waits for them, and re-layouts  2.2 us (2%)
    pallas_call x1, Pallas kernels, body(): pl.pallas_call(functools.partial(kernel, dims), out_shape=(jax.ShapeDtype...  102 us
    unnamed x2, local copies, waits for them, and re-layouts  2.2 us

profile of v2, /device:TPU:0, one launch (start us, length us, event | category | flops | bytes accessed | tf_op | source)
XLA Modules:
  0.0 104.5 jit_solution(5984933569584125074)
XLA Ops:
  0.6 101.7 %shard_map.104 = (bf16[16,256,256]{2,1,0:T(8,128)(2,1)S(1)}, bf16[6,256,256]{2,1,0:T(8,128)(2,1)S(1)}) custom-call(s32[2,8]{1,0:T(2,128)} %bitcast.11, s32[4,8]{1,0:T(4,128)} %bitcast.9, s32[6,2,8]{2,1,0:T(2,128)} %bitcast.8, s32[1,8]{1,0:T(1,128)} %peer_hbm.1, s32[1,2]{1,0:T(1,128)} %slab_hbm.1, s32[2,2,8]{2,1,0:T(2,128)} %bitcast.10, ...), custom_call_target="tpu_custom_call" | custom-call | tf_op jit(solution)/shard_map/pallas_call | solution.py:461
  102.3 1.3 %copy.13 = bf16[8,2,256,256]{3,2,1,0:T(8,128)(2,1)} copy(bf16[8,2,256,256]{3,2,1,0:T(8,128)(2,1)S(1)} %bitcast.6) | data formatting | bytes 4194304
  103.7 0.9 copy.14

commit v3 on v2

--- a/solution.py
+++ b/solution.py
@@ -149,7 +149,7 @@
 
     def post_rows(step, s):
         def post(turn, carry):
-            offset = 1 + (2 * turn + 1) % (group - 1)
+            offset = 1 + (turn + 5) % (group - 1)
             target = (me + offset) % group
             for p in range(peers):
                 row = peer_ref[0, target * peers + p]
@@ -176,7 +176,7 @@
 
     def arrive(step, s):
         def finish(turn, carry):
-            peer_copy(step, s, 1 + (2 * turn + 1) % (group - 1)).wait()
+            peer_copy(step, s, 1 + (turn + 5) % (group - 1)).wait()
             return carry
 
         lax.fori_loop(0, group - 1, finish, 0)
@@ -267,7 +267,7 @@
 
     core = me % 2
     half = group * owned // 2
-    grain = owned // 2 if owned % 2 == 0 else owned
+    grain = owned
 
     def invert(at, carry):
         place = at // owned
@@ -407,6 +407,23 @@
                 half_copy(step, s, chunk).wait_send()
     for store in stores:
         store.wait()
+
+
+def deliver(pieces, smooth_ref, coarse_ref, smooth_out, coarse_out, sem):
+    copies = []
+    for which, (source, target) in enumerate(((smooth_ref, smooth_out), (coarse_ref, coarse_out))):
+        step = pl.cdiv(source.shape[0], pieces)
+        for piece, at in enumerate(range(0, source.shape[0], step)):
+            window = pl.ds(at, min(step, source.shape[0] - at))
+            copies.append(
+                pltpu.make_async_copy(
+                    source.at[window], target.at[window], sem.at[which, piece]
+                )
+            )
+    for copy in copies:
+        copy.start()
+    for copy in copies:
+        copy.wait()
 
 
 def body(
@@ -496,6 +513,15 @@
             collective_id=0, has_side_effects=True, vmem_limit_bytes=grant
         ),
     )(*[pltpu.with_memory_space_constraint(x, pltpu.HBM) for x in tables + arrays])
+    pieces = 4
+    results = [pltpu.with_memory_space_constraint(x, pltpu.VMEM) for x in (smoothed, coarse)]
+    smoothed, coarse = pl.pallas_call(
+        functools.partial(deliver, pieces),
+        out_shape=tuple(jax.ShapeDtypeStruct(x.shape, x.dtype) for x in (smoothed, coarse)),
+        in_specs=[pl.BlockSpec(memory_space=pltpu.VMEM)] * 2,
+        out_specs=(anywhere, anywhere),
+        scratch_shapes=[pltpu.SemaphoreType.DMA((2, pieces))],
+    )(*results)
     return smoothed.reshape(tentative.shape), coarse
 
 

time: 105 us -> 103 us (0.981)
  local copies, waits for them, and re-layouts: 2.2 us -> 0 us
    unnamed x2 -> x0, local copies, waits for them, and re-layouts: 2.2 us -> none
    pallas_call x0 -> x1, Pallas kernels: none -> 1.64 us  [body(): pl.pallas_call(functools.partial(deliver, pieces), out_shape=tuple((jax.S...]
where the time goes in v3:
time: 103 us
  Pallas kernels  102 us (99%)
    pallas_call x1, Pallas kernels, body(): pl.pallas_call(functools.partial(kernel, dims), out_shape=(jax.ShapeDtype...  101 us

profile of v3, /device:TPU:0, one launch (start us, length us, event | category | flops | bytes accessed | tf_op | source)
XLA Modules:
  0.0 102.9 jit_solution(7770836039300045321)
XLA Ops:
  0.6 100.6 %shard_map.104 = (bf16[16,256,256]{2,1,0:T(8,128)(2,1)S(1)}, bf16[6,256,256]{2,1,0:T(8,128)(2,1)S(1)}) custom-call(s32[2,8]{1,0:T(2,128)} %bitcast.10, s32[4,8]{1,0:T(4,128)} %bitcast.8, s32[6,2,8]{2,1,0:T(2,128)} %bitcast.7, s32[1,8]{1,0:T(1,128)} %peer_hbm.1, s32[1,2]{1,0:T(1,128)} %slab_hbm.1, s32[2,2,8]{2,1,0:T(2,128)} %bitcast.9, ...), custom_call_target="tpu_custom_call" | custom-call | tf_op jit(solution)/shard_map/pallas_call | solution.py:478
  101.3 1.6 %shard_map.105 = (bf16[16,256,256]{2,1,0:T(8,128)(2,1)}, bf16[6,256,256]{2,1,0:T(8,128)(2,1)}) custom-call(bf16[16,256,256]{2,1,0:T(8,128)(2,1)S(1)} %get-tuple-element.6.smooth_ref, bf16[6,256,256]{2,1,0:T(8,128)(2,1)S(1)} %get-tuple-element.7.coarse_ref), custom_call_target="tpu_custom_call" | custom-call | tf_op jit(solution)/shard_map/pallas_call | solution.py:518

commit v4 on v3

--- a/solution.py
+++ b/solution.py
@@ -1,4 +1,5 @@
 import functools
+import math
 
 import jax
 import jax.numpy as jnp
@@ -90,14 +91,8 @@
     load_remotes = pltpu.make_async_copy(remote_hbm, remote_ref, index_sem.at[4])
     load_slots = pltpu.make_async_copy(slots_hbm, slots_ref, index_sem.at[5])
     load_rows(0).start()
-    for load in (load_peers, load_slabs, load_matches, load_locals, load_remotes, load_slots):
-        load.start()
-    for s in range(1, STRIPES):
-        load_rows(s).start()
-    load_operator = pltpu.make_async_copy(operator_hbm, operator, load_sem.at[0])
-    load_operator.start()
-    load_diagonal = pltpu.make_async_copy(diagonal_hbm, diagonal, load_sem.at[1])
-    load_diagonal.start()
+    load_peers.start()
+    load_slabs.start()
 
     barrier = pltpu.get_barrier_semaphore()
 
@@ -117,12 +112,14 @@
     def _():
         pl.semaphore_signal(barrier, inc=1, device_id=(gx + 1, me), device_id_type=MESH)
 
-    zero = jnp.zeros((width, columns), jnp.bfloat16)
-    for s in range(STRIPES):
-        owns[s][own_zero] = zero
-        for rem in rems:
-            rem[s][rem_zero] = zero
-        partial[s, count] = zero
+    for s in range(1, STRIPES):
+        load_rows(s).start()
+    for load in (load_matches, load_locals, load_remotes, load_slots):
+        load.start()
+    load_operator = pltpu.make_async_copy(operator_hbm, operator, load_sem.at[0])
+    load_operator.start()
+    load_diagonal = pltpu.make_async_copy(diagonal_hbm, diagonal, load_sem.at[1])
+    load_diagonal.start()
     neighbours = jnp.where(has_below, 1, 0) + jnp.where(has_above, 1, 0)
     pl.semaphore_wait(barrier, group - 1 + neighbours)
 
@@ -248,16 +245,15 @@
     def turn_row(row, carry):
         for n in range(kp):
             for s in range(STRIPES):
-                turned[row * kp + n, pl.ds(s * columns, columns)] = owns[s][row * kp + n].T
+                turned[row, pl.ds(n * width + s * columns, columns)] = owns[s][row * kp + n].T
         return carry
 
     def partial_rows(step, s):
         def partial_row(row, carry):
             image = image_of(row, step, s)
+            stack = jnp.dot(turned[row], image, preferred_element_type=jnp.float32)
             for n in range(kp):
-                blocks = jnp.dot(
-                    turned[row * kp + n], image, preferred_element_type=jnp.float32
-                ).astype(jnp.bfloat16)
+                blocks = stack[n * width : (n + 1) * width].astype(jnp.bfloat16)
                 for m in range(kp):
                     at = (row * kp + n) * kp + m
                     partial[s, at] = blocks[:, m * columns : (m + 1) * columns]
@@ -359,6 +355,12 @@
     load_slabs.wait()
     load_rows(0).wait()
     post_rows(0, 0)
+    zero = jnp.zeros((width, columns), jnp.bfloat16)
+    for s in range(STRIPES):
+        owns[s][own_zero] = zero
+        for rem in rems:
+            rem[s][rem_zero] = zero
+        partial[s, count] = zero
     load_matches.wait()
     load_locals.wait()
     load_remotes.wait()
@@ -464,17 +466,23 @@
     anywhere = pl.BlockSpec(memory_space=pl.ANY)
     half = group * owned // 2
     remote_count = (group * peers + 2 * halo) * kp
-    scratch_blocks = (
-        (kl + ko + 1) * rows
-        + rows * kp * 2
-        + 3 * remote_count
-        + 2 * rows * kp
-        + count
-        + 4 * half
-        + owned
-        + 4
+    vmem = [
+        pltpu.VMEM(operator_blocks.shape, jnp.bfloat16),
+        pltpu.VMEM((rows, width, width), jnp.bfloat16),
+        blocks(remote_count),
+        pltpu.VMEM((STRIPES, rows, width, kp * columns), jnp.float32),
+        pltpu.VMEM((rows, kp * width, width), jnp.bfloat16),
+        blocks(count + 1),
+        blocks(half),
+        blocks(half),
+    ]
+    striped = [pltpu.VMEM((rows * kp + 1, width, columns), jnp.bfloat16)] * STRIPES
+    striped += [pltpu.VMEM((remote_count + 1, width, columns), jnp.bfloat16)] * (2 * STRIPES)
+    landed = [blocks(half >> step) for step in range(bits)]
+    used = sum(
+        math.prod(x.shape) * jnp.dtype(x.dtype).itemsize for x in [*vmem, *striped, *landed]
     )
-    grant = scratch_blocks * width * width * 2 + 3_000_000
+    grant = used + owned * width * width * 2 + (1 << 20)
     smoothed, coarse = pl.pallas_call(
         functools.partial(kernel, dims),
         out_shape=(
@@ -484,20 +492,12 @@
         in_specs=[pl.BlockSpec(memory_space=pltpu.HBM)] * 9,
         out_specs=(anywhere, pl.BlockSpec(memory_space=pltpu.VMEM)),
         scratch_shapes=[
-            pltpu.VMEM(operator_blocks.shape, jnp.bfloat16),
-            pltpu.VMEM((rows, width, width), jnp.bfloat16),
-            blocks(remote_count),
-            pltpu.VMEM((STRIPES, rows, width, kp * columns), jnp.float32),
-            pltpu.VMEM((rows * kp, width, width), jnp.bfloat16),
-            blocks(count + 1),
-            blocks(half),
-            blocks(half),
+            *vmem,
             *[pltpu.SMEM(table.shape, jnp.int32) for table in tables],
             pltpu.SMEM((kl + ko, kp, rows), jnp.int32),
             pltpu.SMEM((2 * half,), jnp.int32),
-            *[pltpu.VMEM((rows * kp + 1, width, columns), jnp.bfloat16)] * STRIPES,
-            *[pltpu.VMEM((remote_count + 1, width, columns), jnp.bfloat16)] * (2 * STRIPES),
-            *[blocks(half >> step) for step in range(bits)],
+            *striped,
+            *landed,
             pltpu.SemaphoreType.DMA((len(tables),)),
             pltpu.SemaphoreType.DMA((2,)),
             pltpu.SemaphoreType.DMA((STRIPES,)),

time: 103 us -> 103 us (level)
  no operation moved by 1% of the time
where the time goes in v4:
time: 103 us
  Pallas kernels  102 us (99%)
    pallas_call x1, Pallas kernels, body(): pl.pallas_call(functools.partial(kernel, dims), out_shape=(jax.ShapeDtype...  101 us

profile of v4, /device:TPU:0, one launch (start us, length us, event | category | flops | bytes accessed | tf_op | source)
XLA Modules:
  0.0 102.9 jit_solution(17359455452805901825)
XLA Ops:
  0.6 100.6 %shard_map.104 = (bf16[16,256,256]{2,1,0:T(8,128)(2,1)S(1)}, bf16[6,256,256]{2,1,0:T(8,128)(2,1)S(1)}) custom-call(s32[2,8]{1,0:T(2,128)} %bitcast.10, s32[4,8]{1,0:T(4,128)} %bitcast.8, s32[6,2,8]{2,1,0:T(2,128)} %bitcast.7, s32[1,8]{1,0:T(1,128)} %peer_hbm.1, s32[1,2]{1,0:T(1,128)} %slab_hbm.1, s32[2,2,8]{2,1,0:T(2,128)} %bitcast.9, ...), custom_call_target="tpu_custom_call" | custom-call | tf_op jit(solution)/shard_map/pallas_call | solution.py:486
  101.3 1.6 %shard_map.105 = (bf16[16,256,256]{2,1,0:T(8,128)(2,1)}, bf16[6,256,256]{2,1,0:T(8,128)(2,1)}) custom-call(bf16[16,256,256]{2,1,0:T(8,128)(2,1)S(1)} %get-tuple-element.6.smooth_ref, bf16[6,256,256]{2,1,0:T(8,128)(2,1)S(1)} %get-tuple-element.7.coarse_ref), custom_call_target="tpu_custom_call" | custom-call | tf_op jit(solution)/shard_map/pallas_call | solution.py:518

commit v5 on v4

--- a/solution.py
+++ b/solution.py
@@ -146,7 +146,7 @@
 
     def post_rows(step, s):
         def post(turn, carry):
-            offset = 1 + (turn + 5) % (group - 1)
+            offset = 1 + turn
             target = (me + offset) % group
             for p in range(peers):
                 row = peer_ref[0, target * peers + p]
@@ -173,7 +173,7 @@
 
     def arrive(step, s):
         def finish(turn, carry):
-            peer_copy(step, s, 1 + (turn + 5) % (group - 1)).wait()
+            peer_copy(step, s, 1 + turn).wait()
             return carry
 
         lax.fori_loop(0, group - 1, finish, 0)
@@ -381,6 +381,10 @@
         for s in stripes:
             arrive(step, s)
             smooth_rows(step, s)
+            if s == STRIPES - 1:
+                local_rows(s)
+                if step == 1:
+                    lax.fori_loop(0, rows, turn_row, 0)
             post_rows(step + 1, s)
             if step == 1:
                 store = pltpu.make_async_copy(
@@ -390,8 +394,8 @@
                 )
                 store.start()
                 stores.append(store)
-            local_rows(s)
-    lax.fori_loop(0, rows, turn_row, 0)
+            if s < STRIPES - 1:
+                local_rows(s)
 
     for s in stripes:
         if s > 0:

time: 103 us -> 103 us (level)
  no operation moved by 1% of the time
where the time goes in v5:
time: 103 us
  Pallas kernels  102 us (99%)
    pallas_call x1, Pallas kernels, body(): pl.pallas_call(functools.partial(kernel, dims), out_shape=(jax.ShapeDtype...  101 us

profile of v5, /device:TPU:0, one launch (start us, length us, event | category | flops | bytes accessed | tf_op | source)
XLA Modules:
  0.0 102.8 jit_solution(3062866742782938326)
XLA Ops:
  0.6 100.5 %shard_map.104 = (bf16[16,256,256]{2,1,0:T(8,128)(2,1)S(1)}, bf16[6,256,256]{2,1,0:T(8,128)(2,1)S(1)}) custom-call(s32[2,8]{1,0:T(2,128)} %bitcast.10, s32[4,8]{1,0:T(4,128)} %bitcast.8, s32[6,2,8]{2,1,0:T(2,128)} %bitcast.7, s32[1,8]{1,0:T(1,128)} %peer_hbm.1, s32[1,2]{1,0:T(1,128)} %slab_hbm.1, s32[2,2,8]{2,1,0:T(2,128)} %bitcast.9, ...), custom_call_target="tpu_custom_call" | custom-call | tf_op jit(solution)/shard_map/pallas_call | solution.py:490
  101.2 1.6 %shard_map.105 = (bf16[16,256,256]{2,1,0:T(8,128)(2,1)}, bf16[6,256,256]{2,1,0:T(8,128)(2,1)}) custom-call(bf16[16,256,256]{2,1,0:T(8,128)(2,1)S(1)} %get-tuple-element.6.smooth_ref, bf16[6,256,256]{2,1,0:T(8,128)(2,1)S(1)} %get-tuple-element.7.coarse_ref), custom_call_target="tpu_custom_call" | custom-call | tf_op jit(solution)/shard_map/pallas_call | solution.py:522

commit v6 on v5

--- a/solution.py
+++ b/solution.py
@@ -155,7 +155,6 @@
             peer_copy(step, s, offset).start()
             return carry
 
-        lax.fori_loop(0, group - 1, post, 0)
         for way, present in enumerate((has_above, has_below)):
 
             @pl.when(present)
@@ -166,6 +165,7 @@
                         send[s, slab_at + way * slab_span + h * kp + n] = owns[s][row * kp + n]
                 slab_copy(step, s, way).start()
 
+        lax.fori_loop(0, group - 1, post, 0)
         for p in range(peers):
             row = peer_ref[0, me * peers + p]
             for n in range(kp):
@@ -368,10 +368,10 @@
     for s in stripes[1:]:
         load_rows(s).wait()
     load_operator.wait()
-    for s in stripes:
-        local_rows(s)
+    local_rows(0)
     for s in stripes[1:]:
         post_rows(0, s)
+        local_rows(s)
     load_slots.wait()
     lax.fori_loop(0, group * owned, invert, 0)
     load_diagonal.wait()

time: 103 us -> 103 us (level)
  no operation moved by 1% of the time
where the time goes in v6:
time: 103 us
  Pallas kernels  102 us (99%)
    pallas_call x1, Pallas kernels, body(): pl.pallas_call(functools.partial(kernel, dims), out_shape=(jax.ShapeDtype...  101 us

profile of v6, /device:TPU:0, one launch (start us, length us, event | category | flops | bytes accessed | tf_op | source)
XLA Modules:
  0.0 102.8 jit_solution(11287594201527538985)
XLA Ops:
  0.6 100.6 %shard_map.104 = (bf16[16,256,256]{2,1,0:T(8,128)(2,1)S(1)}, bf16[6,256,256]{2,1,0:T(8,128)(2,1)S(1)}) custom-call(s32[2,8]{1,0:T(2,128)} %bitcast.10, s32[4,8]{1,0:T(4,128)} %bitcast.8, s32[6,2,8]{2,1,0:T(2,128)} %bitcast.7, s32[1,8]{1,0:T(1,128)} %peer_hbm.1, s32[1,2]{1,0:T(1,128)} %slab_hbm.1, s32[2,2,8]{2,1,0:T(2,128)} %bitcast.9, ...), custom_call_target="tpu_custom_call" | custom-call | tf_op jit(solution)/shard_map/pallas_call | solution.py:490
  101.2 1.6 %shard_map.105 = (bf16[16,256,256]{2,1,0:T(8,128)(2,1)}, bf16[6,256,256]{2,1,0:T(8,128)(2,1)}) custom-call(bf16[16,256,256]{2,1,0:T(8,128)(2,1)S(1)} %get-tuple-element.6.smooth_ref, bf16[6,256,256]{2,1,0:T(8,128)(2,1)S(1)} %get-tuple-element.7.coarse_ref), custom_call_target="tpu_custom_call" | custom-call | tf_op jit(solution)/shard_map/pallas_call | solution.py:522

commit v7 on v5

--- a/solution.py
+++ b/solution.py
@@ -517,7 +517,7 @@
             collective_id=0, has_side_effects=True, vmem_limit_bytes=grant
         ),
     )(*[pltpu.with_memory_space_constraint(x, pltpu.HBM) for x in tables + arrays])
-    pieces = 4
+    pieces = 1
     results = [pltpu.with_memory_space_constraint(x, pltpu.VMEM) for x in (smoothed, coarse)]
     smoothed, coarse = pl.pallas_call(
         functools.partial(deliver, pieces),

time: 103 us -> 103 us (level)
  no operation moved by 1% of the time
where the time goes in v7:
time: 103 us
  Pallas kernels  102 us (99%)
    pallas_call x1, Pallas kernels, body(): pl.pallas_call(functools.partial(kernel, dims), out_shape=(jax.ShapeDtype...  101 us

profile of v7, /device:TPU:0, one launch (start us, length us, event | category | flops | bytes accessed | tf_op | source)
XLA Modules:
  0.0 102.8 jit_solution(8580177356238317991)
XLA Ops:
  0.6 100.5 %shard_map.104 = (bf16[16,256,256]{2,1,0:T(8,128)(2,1)S(1)}, bf16[6,256,256]{2,1,0:T(8,128)(2,1)S(1)}) custom-call(s32[2,8]{1,0:T(2,128)} %bitcast.10, s32[4,8]{1,0:T(4,128)} %bitcast.8, s32[6,2,8]{2,1,0:T(2,128)} %bitcast.7, s32[1,8]{1,0:T(1,128)} %peer_hbm.1, s32[1,2]{1,0:T(1,128)} %slab_hbm.1, s32[2,2,8]{2,1,0:T(2,128)} %bitcast.9, ...), custom_call_target="tpu_custom_call" | custom-call | tf_op jit(solution)/shard_map/pallas_call | solution.py:490
  101.2 1.6 %shard_map.105 = (bf16[16,256,256]{2,1,0:T(8,128)(2,1)}, bf16[6,256,256]{2,1,0:T(8,128)(2,1)}) custom-call(bf16[16,256,256]{2,1,0:T(8,128)(2,1)S(1)} %get-tuple-element.6.smooth_ref, bf16[6,256,256]{2,1,0:T(8,128)(2,1)S(1)} %get-tuple-element.7.coarse_ref), custom_call_target="tpu_custom_call" | custom-call | tf_op jit(solution)/shard_map/pallas_call | solution.py:522
